TPU v7x, 256 devices: a whole 4x4x8 slice. The times are simulated.
256 devices in a mesh: gx: 4 (over x), gy: 8 (over y, core), gz: 8 (over z).
Axes of the slice: x: 4, y: 4, z: 8, core: 2. Of those that a mesh axis runs over, the one named last changes fastest.
Arguments:
- fields: float32 [3, 64, 128, 1024], P(None, 'gx', 'gy', 'gz'), may hold values from -6 to 6
- diffusivity: float32 [64, 128, 1024], P('gx', 'gy', 'gz'), may hold values from 0.03 to 0.15
- velocity: float32 [3, 64, 128, 1024], P(None, 'gx', 'gy', 'gz'), may hold values from -2.4 to 2.4
- stored_snapshots: bfloat16 [127, 786432], P(None, ('gx', 'gy', 'gz')), may hold values from -36 to 36
- sample_index: int32 [262144], P(('gx', 'gy', 'gz')), may hold values from 0 to 32767, as said below
Outputs:
- new_fields: float32 [3, 64, 128, 1024], P(None, 'gx', 'gy', 'gz')
- snapshot_r: float32 [128, 128], replicated
Inputs may be any that keep to these rules, and one draw needn't show every extreme that they name: `sample_index`: entry k of a tile's list lies between k * 32 and (k + 1) * 32 - 1.
All inputs are finite; a program needn't handle non-finite values.
Results may differ from a plain program's by a relative error of at most 0.0003.
Values sent between devices are 32-bit elements; how exact they have to be, the bound alone decides.
A program may use at most 64 MiB of HBM per device.

v0:
```python
import jax
import jax.numpy as jnp
from jax import lax
from jax.sharding import PartitionSpec as P


def with_halo(array, sides, width):
    for axis, dim in sides:
        devices, length = (lax.axis_size(axis), array.shape[dim])
        up = [(i, (i + 1) % devices) for i in range(devices - 1)]
        down = [(j, i) for i, j in up]
        last = lax.slice_in_dim(array, length - width, length, axis=dim)
        first = lax.slice_in_dim(array, 0, width, axis=dim)
        before = lax.ppermute(last, axis, up)
        after = lax.ppermute(first, axis, down)
        array = jnp.concatenate([before, array, after], axis=dim)
    return array


def face_term(center_u, center_k, plus_u, plus_k, plus_v, minus_u, minus_k, minus_v):
    return (
        0.5 * (plus_k + center_k) * (plus_u - center_u)
        - 0.5 * (center_k + minus_k) * (center_u - minus_u)
        - 0.5 * (plus_v * plus_u - minus_v * minus_u)
    )


def upper_factor(gram):
    return jnp.linalg.cholesky(gram).T


def inner_rows(left, right):
    return lax.dot_general(
        left, right, (((1,), (1,)), ((), ())), preferred_element_type=jnp.float32
    )


def per_device(fields, diffusivity, velocity, stored_snapshots, sample_index):
    total_rows = (
        stored_snapshots.shape[1] * lax.axis_size("gx") * lax.axis_size("gy") * lax.axis_size("gz")
    )
    stacked = jnp.concatenate([fields, velocity, diffusivity[None]], 0)
    padded = with_halo(stacked, (("gx", 1), ("gy", 2), ("gz", 3)), 1)
    padded_u = padded[0:3]
    padded_v = padded[3:6]
    padded_k = padded[6]
    inner = (slice(1, -1), slice(1, -1), slice(1, -1))
    terms = []
    for dim in range(3):
        upper = list(inner)
        lower = list(inner)
        upper[dim] = slice(2, None)
        lower[dim] = slice(None, -2)
        upper = tuple(upper)
        lower = tuple(lower)
        terms.append(
            face_term(
                fields,
                diffusivity,
                padded_u[(slice(None),) + upper],
                padded_k[upper],
                padded_v[dim][upper],
                padded_u[(slice(None),) + lower],
                padded_k[lower],
                padded_v[dim][lower],
            )
        )
    new_fields = fields + (terms[0] + terms[1] + terms[2])
    flat_cells = new_fields.reshape(3, -1)
    sampled = jnp.take(flat_cells, sample_index, axis=1)
    new_column = sampled.reshape(1, -1).astype(jnp.bfloat16)
    snapshot_block = jnp.concatenate([stored_snapshots, new_column], 0)
    local_gram = inner_rows(snapshot_block, snapshot_block) / float(total_rows)
    whole_gram = lax.psum(local_gram, ("gx", "gy", "gz"))
    snapshot_r = upper_factor(whole_gram)
    return (new_fields, snapshot_r)


def solution(mesh):
    placed = (
        P(None, "gx", "gy", "gz"),
        P("gx", "gy", "gz"),
        P(None, "gx", "gy", "gz"),
        P(None, ("gx", "gy", "gz")),
        P(("gx", "gy", "gz")),
    )
    return jax.shard_map(
        per_device,
        mesh=mesh,
        in_specs=placed,
        out_specs=(P(None, "gx", "gy", "gz"), P()),
        check_vma=False,
    )
```

profile of v0, /device:TPU:1, one launch (start us, length us, event | category | flops | bytes accessed | tf_op | source)
XLA Modules:
  0.0 335.2 jit_solution(9069121309860138379)
XLA Ops:
  7.2 0.0 copy-start.3
  7.2 0.0 copy-start
  7.2 0.0 copy-start.1
  7.2 0.0 copy-start.11
  7.2 0.0 all-reduce.2.cloned.1.call-start
  7.3 0.9 pad_maximum_fusion.25
  8.2 3.9 %collective-permute-start = (f32[7,1,16,128]{3,2,1,0:T(8,128)S(1)}, f32[7,1,16,128]{3,2,1,0:T(8,128)S(1)}, u32[]{:S(2)}, u32[]{:S(2)}) collective-permute-start(f32[7,1,16,128]{3,2,1,0:T(8,128)S(1)} %get-tuple-element.18), channel_id=1, source_target_pairs={{0,64},{64,128},{128,192},{1,65},{65,129},{129,193},{2,66},{66,130... | collective-permute-start | bytes 172040 | tf_op jit(solution)/shard_map/ppermute | solution.py:14
  12.1 1.3 collective-permute-start.1
  13.4 0.0 collective-permute-done
  13.4 3.6 %collective-permute-done.1 = f32[7,1,16,128]{3,2,1,0:T(8,128)S(1)} collective-permute-done((f32[7,1,16,128]{3,2,1,0:T(8,128)S(1)}, f32[7,1,16,128]{3,2,1,0:T(8,128)S(1)}, u32[]{:S(2)}, u32[]{:S(2)}) %collective-permute-start.1) | collective-permute-done | bytes 57376 | tf_op jit(solution)/shard_map/ppermute | solution.py:15
  17.0 0.0 copy-start.5
  17.0 1.4 pad_maximum_fusion.22
  18.4 5.2 %collective-permute-start.2 = (f32[7,18,1,128]{3,2,1,0:T(1,128)S(1)}, f32[7,18,1,128]{3,2,1,0:T(1,128)S(1)}, u32[]{:S(2)}, u32[]{:S(2)}) collective-permute-start(f32[7,18,1,128]{3,2,1,0:T(1,128)S(1)} %get-tuple-element.16), channel_id=1, source_target_pairs={{0,8},{8,16},{16,24},{24,32},{32,40},{40,48},{48,56},{1,9},{9,17},... | collective-permute-start | bytes 193544 | tf_op jit(solution)/shard_map/ppermute | solution.py:14
  23.6 1.9 collective-permute-start.3
  25.6 0.0 copy-done.11
  25.6 0.0 collective-permute-done.2
  25.6 0.0 copy-start.7
  25.6 3.6 %collective-permute-done.3 = f32[7,18,1,128]{3,2,1,0:T(1,128)S(1)} collective-permute-done((f32[7,18,1,128]{3,2,1,0:T(1,128)S(1)}, f32[7,18,1,128]{3,2,1,0:T(1,128)S(1)}, u32[]{:S(2)}, u32[]{:S(2)}) %collective-permute-start.3) | collective-permute-done | bytes 64544 | tf_op jit(solution)/shard_map/ppermute | solution.py:15
  29.2 0.0 copy-done.5
  29.2 0.0 copy-done.7
  29.2 0.0 copy-start.9
  29.2 0.6 copy-done.9
  29.8 0.0 copy-done.3
  29.8 0.0 copy-done
  29.8 0.0 copy-done.1
  29.8 0.3 pad_maximum_fusion.1
  30.1 0.5 fusion.27
  30.6 1.6 copy.38
  32.2 3.5 %collective-permute-start.4 = (f32[7,18,18,1]{2,0,3,1:T(8,128)}, f32[7,18,18,1]{2,0,3,1:T(8,128)S(1)}, u32[]{:S(2)}, u32[]{:S(2)}) collective-permute-start(f32[7,18,18,1]{2,0,3,1:T(8,128)} %copy.38), channel_id=1, source_target_pairs={{0,1},{1,2},{2,3},{3,4},{4,5},{5,6},{6,7},{8,9},{9,10},{10,11},{11... | collective-permute-start | bytes 27224 | tf_op jit(solution)/shard_map/ppermute | solution.py:14
  35.7 1.0 copy.39
  36.7 1.5 collective-permute-start.5
  38.1 0.6 compare_and_fusion
  38.7 0.0 collective-permute-done.4
  38.7 0.9 copy.40
  39.6 2.4 collective-permute-done.5
  42.1 1.8 copy.41
  43.8 4.9 %pad_maximum_fusion = f32[7,18,18,130]{3,2,1,0:T(8,128)S(1)} fusion(f32[7,18,18,1]{3,2,1,0:T(8,128)S(1)} %copy.41, f32[7,18,1,128]{3,2,1,0:T(1,128)} %copy-done.9, f32[7,1,16,128]{3,2,1,0:T(8,128)} %copy-done.5, f32[1,16,16,128]{3,2,1,0:T(8,128)} %bitcast.24, f32[3,16,16,128]{3,2,1,0:T(8,128)} %param.7, f32[3,16,16,128]{3,2,1,0:T(8,128)S(1)} %copy-done, ...), kind=kLoop, calls=%fused_computation.1 | loop fusion | flops 2358720 | bytes 2358720 | tf_op jit(solution)/shard_map/concatenate | solution.py:16
  48.8 0.0 copy-start.4
  48.8 0.2 slice_bitcast_fusion.2
  48.9 0.7 copy-done.4
  49.7 0.0 copy-start.2
  49.7 0.0 copy-start.6
  49.7 0.3 fusion.23
  50.0 0.2 fusion.29
  50.2 0.5 copy-done.2
  50.7 0.0 copy-done.6
  50.7 0.0 copy-done.8
  50.7 0.0 copy-done.10
  50.7 1.5 add_add_fusion
  52.2 7.4 %copy.44 = bf16[3,16,16,128]{0,3,2,1:T(8,128)(2,1)} copy(f32[3,16,16,128]{3,2,1,0:T(8,128)} %add_add_fusion) | data formatting | bytes 589824 | tf_op jit(solution)/shard_map/add | solution.py:68
  59.6 7.3 %gather_fusion = bf16[1024,3]{1,0:T(8,128)(2,1)S(1)} fusion(bf16[3,32768]{0,1:T(8,128)(2,1)} %bitcast.21, s32[1024]{0:T(1024)S(1)} %fusion.25), kind=kCustom, calls=%fused_computation | custom fusion | bytes 16384 | tf_op jit(solution)/shard_map/jit(_take)/gather | solution.py:70
  66.9 0.0 copy-done.12
  66.9 0.2 fusion.17
  67.1 0.1 copy.45
  67.3 0.0 copy-done.13
  67.3 1.0 convolution_multiply_fusion
  68.3 0.0 all-reduce.2.cloned.1.call-update
  68.3 244.4 %all-reduce.2.cloned.1.call-done = f32[128,128]{0,1:T(8,128)} async-done(((f32[128,128]{0,1:T(8,128)}), f32[128,128]{0,1:T(8,128)}) %all-reduce.2.cloned.1.call-update) | async-done | bytes 65552 | tf_op jit(solution)/shard_map/psum | solution.py:74
  312.8 0.9 copy.47
  313.7 0.9 fusion.24
  314.6 11.7 %cholesky.18 = f32[128,128]{1,0:T(8,128)S(1)} custom-call(f32[128,128]{1,0:T(8,128)S(1)} %fusion.24), custom_call_target="Cholesky" | custom-call | tf_op jit(solution)/shard_map/jit(cholesky)/cholesky | solution.py:29
  326.3 0.6 compare_reduce_fusion
  327.0 0.7 select_bitcast_fusion
  327.6 0.7 copy.48
  (7 shorter events, 0.1 us)
Async XLA Ops:
  7.2 22.7 %copy-start.3 = (f32[16,16,128]{2,1,0:T(8,128)S(1)}, f32[16,16,128]{2,1,0:T(8,128)}, u32[]{:S(2)}) copy-start(f32[16,16,128]{2,1,0:T(8,128)} %param.6) | copy-start | bytes 393220
  7.2 22.7 %copy-start = (f32[3,16,16,128]{3,2,1,0:T(8,128)S(1)}, f32[3,16,16,128]{3,2,1,0:T(8,128)}, u32[]{:S(2)}) copy-start(f32[3,16,16,128]{3,2,1,0:T(8,128)} %param.5) | copy-start | bytes 1179652
  7.2 22.7 %copy-start.1 = (f32[3,16,16,128]{3,2,1,0:T(8,128)S(1)}, f32[3,16,16,128]{3,2,1,0:T(8,128)}, u32[]{:S(2)}) copy-start(f32[3,16,16,128]{3,2,1,0:T(8,128)} %param.7) | copy-start | bytes 1179652
  7.2 18.4 %copy-start.11 = (s32[1024]{0:T(1024)S(1)}, s32[1024]{0:T(1024)}, u32[]{:S(2)}) copy-start(s32[1024]{0:T(1024)} %param.9) | copy-start | bytes 12292
  7.2 305.6 %all-reduce.2.cloned.1.call-start = ((), (), s32[]{:S(2)}) async-start(), calls=%async_computation | async-start | bytes 131072 | tf_op jit(solution)/shard_map/psum | solution.py:74
  8.2 5.2 %collective-permute-start = (f32[7,1,16,128]{3,2,1,0:T(8,128)S(1)}, f32[7,1,16,128]{3,2,1,0:T(8,128)S(1)}, u32[]{:S(2)}, u32[]{:S(2)}) collective-permute-start(f32[7,1,16,128]{3,2,1,0:T(8,128)S(1)} %get-tuple-element.18), channel_id=1, source_target_pairs={{0,64},{64,128},{128,192},{1,65},{65,129},{129,193},{2,66},{66,130... | collective-permute-start | bytes 172040 | tf_op jit(solution)/shard_map/ppermute | solution.py:14
  12.1 4.9 %collective-permute-start.1 = (f32[7,1,16,128]{3,2,1,0:T(8,128)S(1)}, f32[7,1,16,128]{3,2,1,0:T(8,128)S(1)}, u32[]{:S(2)}, u32[]{:S(2)}) collective-permute-start(f32[7,1,16,128]{3,2,1,0:T(8,128)S(1)} %get-tuple-element.19), channel_id=1, source_target_pairs={{64,0},{128,64},{192,128},{65,1},{129,65},{193,129},{66,2},{130,66... | collective-permute-start | bytes 172040 | tf_op jit(solution)/shard_map/ppermute | solution.py:15
  17.0 12.2 %copy-start.5 = (f32[7,1,16,128]{3,2,1,0:T(8,128)}, f32[7,1,16,128]{3,2,1,0:T(8,128)S(1)}, u32[]{:S(2)}) copy-start(f32[7,1,16,128]{3,2,1,0:T(8,128)S(1)} %collective-permute-done.1) | copy-start | bytes 172036
  18.4 7.2 %collective-permute-start.2 = (f32[7,18,1,128]{3,2,1,0:T(1,128)S(1)}, f32[7,18,1,128]{3,2,1,0:T(1,128)S(1)}, u32[]{:S(2)}, u32[]{:S(2)}) collective-permute-start(f32[7,18,1,128]{3,2,1,0:T(1,128)S(1)} %get-tuple-element.16), channel_id=1, source_target_pairs={{0,8},{8,16},{16,24},{24,32},{32,40},{40,48},{48,56},{1,9},{9,17},... | collective-permute-start | bytes 193544 | tf_op jit(solution)/shard_map/ppermute | solution.py:14
  23.6 5.6 %collective-permute-start.3 = (f32[7,18,1,128]{3,2,1,0:T(1,128)S(1)}, f32[7,18,1,128]{3,2,1,0:T(1,128)S(1)}, u32[]{:S(2)}, u32[]{:S(2)}) collective-permute-start(f32[7,18,1,128]{3,2,1,0:T(1,128)S(1)} %get-tuple-element.17), channel_id=1, source_target_pairs={{8,0},{16,8},{24,16},{32,24},{40,32},{48,40},{56,48},{9,1},{17,9},... | collective-permute-start | bytes 193544 | tf_op jit(solution)/shard_map/ppermute | solution.py:15
  25.6 3.6 %copy-start.7 = (f32[7,18,1,128]{3,2,1,0:T(1,128)}, f32[7,18,1,128]{3,2,1,0:T(1,128)S(1)}, u32[]{:S(2)}) copy-start(f32[7,18,1,128]{3,2,1,0:T(1,128)S(1)} %collective-permute-done.2) | copy-start | bytes 193540
  29.2 0.6 copy-start.9
  32.2 6.5 %collective-permute-start.4 = (f32[7,18,18,1]{2,0,3,1:T(8,128)}, f32[7,18,18,1]{2,0,3,1:T(8,128)S(1)}, u32[]{:S(2)}, u32[]{:S(2)}) collective-permute-start(f32[7,18,18,1]{2,0,3,1:T(8,128)} %copy.38), channel_id=1, source_target_pairs={{0,1},{1,2},{2,3},{3,4},{4,5},{5,6},{6,7},{8,9},{9,10},{10,11},{11... | collective-permute-start | bytes 27224 | tf_op jit(solution)/shard_map/ppermute | solution.py:14
  36.7 5.4 %collective-permute-start.5 = (f32[7,18,18,1]{2,0,3,1:T(8,128)S(1)}, f32[7,18,18,1]{2,0,3,1:T(8,128)}, u32[]{:S(2)}, u32[]{:S(2)}) collective-permute-start(f32[7,18,18,1]{2,0,3,1:T(8,128)S(1)} %copy.39), channel_id=1, source_target_pairs={{1,0},{2,1},{3,2},{4,3},{5,4},{6,5},{7,6},{9,8},{10,9},{11,10},{12... | collective-permute-start | bytes 27224 | tf_op jit(solution)/shard_map/ppermute | solution.py:15
  48.8 0.9 copy-start.4
  49.7 1.0 copy-start.2
  49.7 1.0 copy-start.6
  49.7 1.0 copy-start.8
  49.7 1.0 copy-start.10
  52.2 14.8 %copy-start.12 = (pred[1024]{0:T(1024)(128)(4,1)S(1)}, pred[1024]{0:T(1024)(128)(4,1)}, u32[]{:S(2)}) copy-start(pred[1024]{0:T(1024)(128)(4,1)} %compare_and_fusion) | copy-start | bytes 3076
  52.2 15.1 %copy-start.13 = (bf16[127,3072]{1,0:T(8,128)(2,1)S(1)}, bf16[127,3072]{1,0:T(8,128)(2,1)}, u32[]{:S(2)}) copy-start(bf16[127,3072]{1,0:T(8,128)(2,1)} %param.8) | copy-start | bytes 2340868
Sparse Core Ops, SparseCore 0:
  68.5 244.2 all-reduce.1
where the time goes:
time: 336 us; the launch traced here: 335 us
  waiting for transfers between devices  254 us (76%)
  local copies, waits for them, and re-layouts  24.5 us (7%)
  other arithmetic  24 us (7%)
  starting transfers between devices  17.4 us (5%)
  between operations  14.3 us (4%)
    psum x1, waiting for transfers between devices, per_device(): whole_gram = lax.psum(local_gram, ('gx', 'gy', 'gz'))  244 us
    ppermute x3, starting transfers between devices, with_halo(): before = lax.ppermute(last, axis, up)  12.7 us
    another operation x3, other arithmetic, upper_factor(): return jnp.linalg.cholesky(gram).T  12.4 us
    ppermute x3, waiting for transfers between devices, with_halo(): after = lax.ppermute(first, axis, down)  9.65 us
    add x1, local copies, waits for them, and re-layouts, per_device(): new_fields = fields + (terms[0] + terms[1] + terms[2])  7.41 us
    gather x1, local copies, waits for them, and re-layouts, per_device(): sampled = jnp.take(flat_cells, sample_index, axis=1)  7.34 us
  transfers between devices with their start and end apart: 7, of which 4 were waited for; matrix products, arithmetic and copies ran while one was open for 1% of the time, Pallas kernels for 0%

commit v1 on v0

--- a/solution.py
+++ b/solution.py
@@ -71,7 +71,7 @@
     new_column = sampled.reshape(1, -1).astype(jnp.bfloat16)
     snapshot_block = jnp.concatenate([stored_snapshots, new_column], 0)
     local_gram = inner_rows(snapshot_block, snapshot_block) / float(total_rows)
-    whole_gram = lax.psum(local_gram, ("gx", "gy", "gz"))
+    whole_gram = jnp.sum(lax.all_gather(local_gram, ("gx", "gy", "gz")), 0)
     snapshot_r = upper_factor(whole_gram)
     return (new_fields, snapshot_r)
 

time: 336 us -> 225 us (0.67)
  waiting for transfers between devices: 254 us -> 138 us
  other arithmetic: 24 us -> 29.7 us
    psum x1 -> x0, waiting for transfers between devices: 244 us -> none  [per_device(): whole_gram = lax.psum(local_gram, ('gx', 'gy', 'gz'))]
    all_gather x0 -> x1, waiting for transfers between devices: none -> 128 us  [per_device(): whole_gram = jnp.sum(lax.all_gather(local_gram, ('gx', 'gy', 'gz')), 0)]
    reduce_sum x0 -> x1, other arithmetic: none -> 6.59 us  [per_device(): whole_gram = jnp.sum(lax.all_gather(local_gram, ('gx', 'gy', 'gz')), 0)]
where the time goes in v1:
time: 225 us
  waiting for transfers between devices  138 us (61%)
  other arithmetic  29.7 us (13%)
  local copies, waits for them, and re-layouts  23.6 us (10%)
  starting transfers between devices  18 us (8%)
  between operations  14.3 us (6%)
    all_gather x1, waiting for transfers between devices, per_device(): whole_gram = jnp.sum(lax.all_gather(local_gram, ('gx', 'gy', 'gz')), 0)  128 us
    ppermute x3, starting transfers between devices, with_halo(): before = lax.ppermute(last, axis, up)  13.3 us
    another operation x3, other arithmetic, upper_factor(): return jnp.linalg.cholesky(gram).T  12.4 us
    ppermute x3, waiting for transfers between devices, with_halo(): after = lax.ppermute(first, axis, down)  10.2 us
    add x1, local copies, waits for them, and re-layouts, per_device(): new_fields = fields + (terms[0] + terms[1] + terms[2])  7.39 us
    gather x1, local copies, waits for them, and re-layouts, per_device(): sampled = jnp.take(flat_cells, sample_index, axis=1)  7.34 us
    reduce_sum x1, other arithmetic, per_device(): whole_gram = jnp.sum(lax.all_gather(local_gram, ('gx', 'gy', 'gz')), 0)  6.59 us
    concatenate x2, other arithmetic, with_halo(): array = jnp.concatenate([before, array, after], axis=dim)  5.21 us
  transfers between devices with their start and end apart: 7, of which 4 were waited for; matrix products, arithmetic and copies ran while one was open for 1% of the time, Pallas kernels for 0%

profile of v1, /device:TPU:1, one launch (start us, length us, event | category | flops | bytes accessed | tf_op | source)
XLA Modules:
  0.0 224.6 jit_solution(6000943730295542074)
XLA Ops:
  7.2 0.0 copy-start.1
  7.2 0.0 copy-start
  7.2 0.0 copy-start.3
  7.2 0.0 copy-start.12
  7.2 0.0 all-gather.3.cloned.1.call-start
  7.3 0.9 pad_maximum_fusion.25
  8.1 3.9 %collective-permute-start = (f32[7,1,16,128]{3,2,1,0:T(8,128)S(1)}, f32[7,1,16,128]{3,2,1,0:T(8,128)S(1)}, u32[]{:S(2)}, u32[]{:S(2)}) collective-permute-start(f32[7,1,16,128]{3,2,1,0:T(8,128)S(1)} %get-tuple-element.18), channel_id=1, source_target_pairs={{0,64},{64,128},{128,192},{1,65},{65,129},{129,193},{2,66},{66,130... | collective-permute-start | bytes 172040 | tf_op jit(solution)/shard_map/ppermute | solution.py:14
  12.1 1.3 collective-permute-start.1
  13.4 0.0 collective-permute-done
  13.4 3.6 %collective-permute-done.1 = f32[7,1,16,128]{3,2,1,0:T(8,128)S(1)} collective-permute-done((f32[7,1,16,128]{3,2,1,0:T(8,128)S(1)}, f32[7,1,16,128]{3,2,1,0:T(8,128)S(1)}, u32[]{:S(2)}, u32[]{:S(2)}) %collective-permute-start.1) | collective-permute-done | bytes 57376 | tf_op jit(solution)/shard_map/ppermute | solution.py:15
  17.0 1.4 pad_maximum_fusion.22
  18.4 5.2 %collective-permute-start.2 = (f32[7,18,1,128]{3,2,1,0:T(1,128)S(1)}, f32[7,18,1,128]{3,2,1,0:T(1,128)S(1)}, u32[]{:S(2)}, u32[]{:S(2)}) collective-permute-start(f32[7,18,1,128]{3,2,1,0:T(1,128)S(1)} %get-tuple-element.16), channel_id=1, source_target_pairs={{0,8},{8,16},{16,24},{24,32},{32,40},{40,48},{48,56},{1,9},{9,17},... | collective-permute-start | bytes 193544 | tf_op jit(solution)/shard_map/ppermute | solution.py:14
  23.6 1.9 collective-permute-start.3
  25.5 0.0 copy-done.12
  25.6 0.0 collective-permute-done.2
  25.6 0.0 copy-start.7
  25.6 3.6 %collective-permute-done.3 = f32[7,18,1,128]{3,2,1,0:T(1,128)S(1)} collective-permute-done((f32[7,18,1,128]{3,2,1,0:T(1,128)S(1)}, f32[7,18,1,128]{3,2,1,0:T(1,128)S(1)}, u32[]{:S(2)}, u32[]{:S(2)}) %collective-permute-start.3) | collective-permute-done | bytes 64544 | tf_op jit(solution)/shard_map/ppermute | solution.py:15
  29.2 0.0 copy-done.5
  29.2 0.0 copy-done.7
  29.2 0.0 copy-start.9
  29.2 0.6 copy-done.9
  29.8 0.0 copy-done.1
  29.8 0.0 copy-done
  29.8 0.0 copy-done.3
  29.8 0.3 pad_maximum_fusion.1
  30.1 0.5 fusion.27
  30.6 1.6 copy.36
  32.2 0.0 copy-start.11
  32.2 0.9 copy.35
  33.1 4.2 %collective-permute-start.4 = (f32[7,18,18,1]{2,0,3,1:T(8,128)S(1)}, f32[7,18,18,1]{2,0,3,1:T(8,128)}, u32[]{:S(2)}, u32[]{:S(2)}) collective-permute-start(f32[7,18,18,1]{2,0,3,1:T(8,128)S(1)} %copy.35), channel_id=1, source_target_pairs={{0,1},{1,2},{2,3},{3,4},{4,5},{5,6},{6,7},{8,9},{9,10},{10,11},{11... | collective-permute-start | bytes 27224 | tf_op jit(solution)/shard_map/ppermute | solution.py:14
  37.3 0.0 copy-done.11
  37.3 1.5 collective-permute-start.5
  38.8 0.6 compare_and_fusion
  39.4 3.0 %collective-permute-done.5 = f32[7,18,18,1]{2,0,3,1:T(8,128)S(1)} collective-permute-done((f32[7,18,18,1]{2,0,3,1:T(8,128)S(1)}, f32[7,18,18,1]{2,0,3,1:T(8,128)S(1)}, u32[]{:S(2)}, u32[]{:S(2)}) %collective-permute-start.5) | collective-permute-done | bytes 9104 | tf_op jit(solution)/shard_map/ppermute | solution.py:15
  42.4 0.9 copy.38
  43.3 0.0 collective-permute-done.4
  43.3 1.8 copy.37
  45.0 4.9 %pad_maximum_fusion = f32[7,18,18,130]{3,2,1,0:T(8,128)S(1)} fusion(f32[7,18,18,1]{3,2,1,0:T(8,128)S(1)} %copy.38, f32[7,18,1,128]{3,2,1,0:T(1,128)} %copy-done.9, f32[7,1,16,128]{3,2,1,0:T(8,128)} %copy-done.5, f32[1,16,16,128]{3,2,1,0:T(8,128)} %bitcast.26, f32[3,16,16,128]{3,2,1,0:T(8,128)} %param.7, f32[3,16,16,128]{3,2,1,0:T(8,128)S(1)} %copy-done, ...), kind=kLoop, calls=%fused_computation.1 | loop fusion | flops 2358720 | bytes 2358720 | tf_op jit(solution)/shard_map/concatenate | solution.py:16
  50.0 0.0 copy-start.4
  50.0 0.2 slice_bitcast_fusion.2
  50.1 0.7 copy-done.4
  50.9 0.0 copy-start.2
  50.9 0.3 fusion.23
  51.2 0.2 fusion.29
  51.4 0.5 copy-done.2
  51.9 0.0 copy-done.6
  51.9 0.0 copy-done.8
  51.9 0.0 copy-done.10
  51.9 1.5 add_add_fusion
  53.4 7.4 %copy.41 = bf16[3,16,16,128]{0,3,2,1:T(8,128)(2,1)} copy(f32[3,16,16,128]{3,2,1,0:T(8,128)} %add_add_fusion) | data formatting | bytes 589824 | tf_op jit(solution)/shard_map/add | solution.py:68
  60.8 7.3 %gather_fusion = bf16[1024,3]{1,0:T(8,128)(2,1)S(1)} fusion(bf16[3,32768]{0,1:T(8,128)(2,1)} %bitcast.23, s32[1024]{0:T(1024)S(1)} %fusion.25), kind=kCustom, calls=%fused_computation | custom fusion | bytes 16384 | tf_op jit(solution)/shard_map/jit(_take)/gather | solution.py:70
  68.1 0.0 copy-done.13
  68.1 0.2 fusion.17
  68.3 0.1 copy.42
  68.5 0.0 copy-done.14
  68.5 1.0 convolution_multiply_fusion
  69.5 0.0 all-gather.3.cloned.1.call-update
  69.5 127.8 %all-gather.3.cloned.1.call-done = f32[32768,128]{1,0:T(8,128)} async-done(((f32[128,128]{1,0:T(8,128)}), f32[32768,128]{1,0:T(8,128)}) %all-gather.3.cloned.1.call-update) | async-done | bytes 16777232 | tf_op jit(solution)/shard_map/all_gather | solution.py:74
  197.3 6.6 %reduce_sum.9 = f32[128,128]{1,0:T(8,128)S(1)} reduce(f32[256,128,128]{2,1,0:T(8,128)} %bitcast.22, f32[]{:T(128)} %constant.56.clone.1), dimensions={0}, to_apply=%region_0.1 | reduce | flops 4177920 | bytes 16842756 | tf_op jit(solution)/shard_map/reduce_sum | solution.py:74
  203.9 0.1 copy.43
  204.0 11.7 %cholesky.18 = f32[128,128]{1,0:T(8,128)S(1)} custom-call(f32[128,128]{1,0:T(8,128)S(1)} %fusion.24), custom_call_target="Cholesky" | custom-call | tf_op jit(solution)/shard_map/jit(cholesky)/cholesky | solution.py:29
  215.8 0.6 compare_reduce_fusion
  216.4 0.7 select_bitcast_fusion
  217.1 0.7 copy.44
  (10 shorter events, 0.1 us)
Async XLA Ops:
  7.2 22.6 %copy-start.1 = (f32[3,16,16,128]{3,2,1,0:T(8,128)S(1)}, f32[3,16,16,128]{3,2,1,0:T(8,128)}, u32[]{:S(2)}) copy-start(f32[3,16,16,128]{3,2,1,0:T(8,128)} %param.7) | copy-start | bytes 1179652
  7.2 22.6 %copy-start = (f32[3,16,16,128]{3,2,1,0:T(8,128)S(1)}, f32[3,16,16,128]{3,2,1,0:T(8,128)}, u32[]{:S(2)}) copy-start(f32[3,16,16,128]{3,2,1,0:T(8,128)} %param.5) | copy-start | bytes 1179652
  7.2 22.6 %copy-start.3 = (f32[16,16,128]{2,1,0:T(8,128)S(1)}, f32[16,16,128]{2,1,0:T(8,128)}, u32[]{:S(2)}) copy-start(f32[16,16,128]{2,1,0:T(8,128)} %param.6) | copy-start | bytes 393220
  7.2 18.3 %copy-start.12 = (s32[1024]{0:T(1024)S(1)}, s32[1024]{0:T(1024)}, u32[]{:S(2)}) copy-start(s32[1024]{0:T(1024)} %param.9) | copy-start | bytes 12292
  7.2 190.1 %all-gather.3.cloned.1.call-start = ((), (), s32[]{:S(2)}) async-start(), calls=%async_computation | async-start | bytes 16842752 | tf_op jit(solution)/shard_map/all_gather | solution.py:74
  8.1 5.2 %collective-permute-start = (f32[7,1,16,128]{3,2,1,0:T(8,128)S(1)}, f32[7,1,16,128]{3,2,1,0:T(8,128)S(1)}, u32[]{:S(2)}, u32[]{:S(2)}) collective-permute-start(f32[7,1,16,128]{3,2,1,0:T(8,128)S(1)} %get-tuple-element.18), channel_id=1, source_target_pairs={{0,64},{64,128},{128,192},{1,65},{65,129},{129,193},{2,66},{66,130... | collective-permute-start | bytes 172040 | tf_op jit(solution)/shard_map/ppermute | solution.py:14
  12.1 4.9 %collective-permute-start.1 = (f32[7,1,16,128]{3,2,1,0:T(8,128)S(1)}, f32[7,1,16,128]{3,2,1,0:T(8,128)S(1)}, u32[]{:S(2)}, u32[]{:S(2)}) collective-permute-start(f32[7,1,16,128]{3,2,1,0:T(8,128)S(1)} %get-tuple-element.19), channel_id=1, source_target_pairs={{64,0},{128,64},{192,128},{65,1},{129,65},{193,129},{66,2},{130,66... | collective-permute-start | bytes 172040 | tf_op jit(solution)/shard_map/ppermute | solution.py:15
  17.0 12.2 %copy-start.5 = (f32[7,1,16,128]{3,2,1,0:T(8,128)}, f32[7,1,16,128]{3,2,1,0:T(8,128)S(1)}, u32[]{:S(2)}) copy-start(f32[7,1,16,128]{3,2,1,0:T(8,128)S(1)} %collective-permute-done.1) | copy-start | bytes 172036
  18.4 7.2 %collective-permute-start.2 = (f32[7,18,1,128]{3,2,1,0:T(1,128)S(1)}, f32[7,18,1,128]{3,2,1,0:T(1,128)S(1)}, u32[]{:S(2)}, u32[]{:S(2)}) collective-permute-start(f32[7,18,1,128]{3,2,1,0:T(1,128)S(1)} %get-tuple-element.16), channel_id=1, source_target_pairs={{0,8},{8,16},{16,24},{24,32},{32,40},{40,48},{48,56},{1,9},{9,17},... | collective-permute-start | bytes 193544 | tf_op jit(solution)/shard_map/ppermute | solution.py:14
  23.6 5.6 %collective-permute-start.3 = (f32[7,18,1,128]{3,2,1,0:T(1,128)S(1)}, f32[7,18,1,128]{3,2,1,0:T(1,128)S(1)}, u32[]{:S(2)}, u32[]{:S(2)}) collective-permute-start(f32[7,18,1,128]{3,2,1,0:T(1,128)S(1)} %get-tuple-element.17), channel_id=1, source_target_pairs={{8,0},{16,8},{24,16},{32,24},{40,32},{48,40},{56,48},{9,1},{17,9},... | collective-permute-start | bytes 193544 | tf_op jit(solution)/shard_map/ppermute | solution.py:15
  25.6 3.6 %copy-start.7 = (f32[7,18,1,128]{3,2,1,0:T(1,128)}, f32[7,18,1,128]{3,2,1,0:T(1,128)S(1)}, u32[]{:S(2)}) copy-start(f32[7,18,1,128]{3,2,1,0:T(1,128)S(1)} %collective-permute-done.2) | copy-start | bytes 193540
  29.2 0.6 copy-start.9
  32.2 5.1 %copy-start.11 = (f32[7,18,18,1]{2,0,3,1:T(8,128)S(1)}, f32[7,18,18,1]{2,0,3,1:T(8,128)}, u32[]{:S(2)}) copy-start(f32[7,18,18,1]{2,0,3,1:T(8,128)} %copy.36) | copy-start | bytes 27220
  33.1 10.2 %collective-permute-start.4 = (f32[7,18,18,1]{2,0,3,1:T(8,128)S(1)}, f32[7,18,18,1]{2,0,3,1:T(8,128)}, u32[]{:S(2)}, u32[]{:S(2)}) collective-permute-start(f32[7,18,18,1]{2,0,3,1:T(8,128)S(1)} %copy.35), channel_id=1, source_target_pairs={{0,1},{1,2},{2,3},{3,4},{4,5},{5,6},{6,7},{8,9},{9,10},{10,11},{11... | collective-permute-start | bytes 27224 | tf_op jit(solution)/shard_map/ppermute | solution.py:14
  37.3 5.1 %collective-permute-start.5 = (f32[7,18,18,1]{2,0,3,1:T(8,128)S(1)}, f32[7,18,18,1]{2,0,3,1:T(8,128)S(1)}, u32[]{:S(2)}, u32[]{:S(2)}) collective-permute-start(f32[7,18,18,1]{2,0,3,1:T(8,128)S(1)} %copy-done.11), channel_id=1, source_target_pairs={{1,0},{2,1},{3,2},{4,3},{5,4},{6,5},{7,6},{9,8},{10,9},{11,10},{12... | collective-permute-start | bytes 27224 | tf_op jit(solution)/shard_map/ppermute | solution.py:15
  50.0 0.9 copy-start.4
  50.9 1.0 copy-start.2
  50.9 1.0 copy-start.6
  50.9 1.0 copy-start.8
  50.9 1.0 copy-start.10
  53.4 14.7 %copy-start.13 = (pred[1024]{0:T(1024)(128)(4,1)S(1)}, pred[1024]{0:T(1024)(128)(4,1)}, u32[]{:S(2)}) copy-start(pred[1024]{0:T(1024)(128)(4,1)} %compare_and_fusion) | copy-start | bytes 3076
  53.4 15.1 %copy-start.14 = (bf16[127,3072]{1,0:T(8,128)(2,1)S(1)}, bf16[127,3072]{1,0:T(8,128)(2,1)}, u32[]{:S(2)}) copy-start(bf16[127,3072]{1,0:T(8,128)(2,1)} %param.8) | copy-start | bytes 2340868
Sparse Core Ops, SparseCore 0:
  69.7 127.6 all-gather.2
